TPU v7x, 512 devices: a whole 4x8x8 slice. The times are simulated.
512 devices in a mesh: grp: 16 (over z, core), blk: 32 (over y, x).
Axes of the slice: x: 4, y: 8, z: 8, core: 2. Of those that a mesh axis runs over, the one named last changes fastest.
Arguments:
- integrals: bfloat16 [32, 2048, 2048], P('blk', None, 'grp'), as said below
- tile_mask: int32 [16, 16], replicated, may hold values from 0 to 1, as said below
- tile_owner: int32 [16], replicated, may hold values from 0 to 15, as said below
- occupied_tiles: bfloat16 [16384, 128], P(('grp', 'blk')), may hold values from -0.1875 to 0.1875
- occupied_offsets: int32 [8], replicated, may hold values from 0 to 15, as said below
- virtual_tiles: bfloat16 [16384, 128], P(('grp', 'blk')), may hold values from -0.1875 to 0.1875
- virtual_offsets: int32 [8], replicated, may hold values from 0 to 15, as said below
Outputs:
- polarizability: float32 [32, 32], P('blk')
Inputs may be any that keep to these rules, and one draw needn't show every extreme that they name: `integrals`: after column slot s is placed at basis tile tile_owner[s], the tensor is symmetric in its two basis indices. `tile_mask`: symmetric, with ones on the diagonal. `tile_owner`: each tile exactly once. `occupied_offsets`: 8 different tile offsets, among them 0 and 15. `virtual_offsets`: 8 different tile offsets, among them 0 and 15.
All inputs are finite; a program needn't handle non-finite values.
Results may differ from a plain program's by a relative error of at most 0.004.
Values may be sent and summed in bfloat16 or wider, within the bound.
A program may use at most 64 MiB of HBM per device.

v0:
```python
import jax
import jax.numpy as jnp
from jax import lax
from jax.sharding import PartitionSpec as P

NT = 16


def body(
    integrals,
    tile_mask,
    tile_owner,
    occupied_tiles,
    occupied_offsets,
    virtual_tiles,
    virtual_offsets,
):
    aux_local, basis_size, local_width = integrals.shape
    tile_width = basis_size // NT
    kcount = occupied_offsets.shape[0]
    local_tiles = local_width // tile_width
    group_index = lax.axis_index("grp")
    local_owner = lax.dynamic_slice_in_dim(tile_owner, group_index * local_tiles, local_tiles)
    matches = (local_owner[None, :, None] == jnp.arange(NT, dtype=jnp.int32)[None, None, :]).astype(
        jnp.int32
    )
    column_mask = jnp.sum(tile_mask[:, None, :] * matches, axis=2)
    blocked = integrals.reshape(aux_local, NT, tile_width, local_tiles, tile_width)
    masked = blocked * column_mask.astype(jnp.bfloat16)[None, :, None, :, None]
    masked = masked.reshape(aux_local, NT, tile_width, local_width)
    occupied_all, virtual_all = (
        lax.all_gather(occupied_tiles, ("grp", "blk"), axis=0, tiled=True),
        lax.all_gather(virtual_tiles, ("grp", "blk"), axis=0, tiled=True),
    )
    occupied_all = occupied_all.reshape(NT, kcount, tile_width, tile_width)
    virtual_all = virtual_all.reshape(NT, kcount, tile_width, tile_width)
    source_rows = (tile_owner[:, None] - occupied_offsets[None, :]) % NT
    partner_rows = (tile_owner[:, None] + virtual_offsets[None, :]) % NT
    virtual_pick = virtual_all[tile_owner]
    occupied_sum = jnp.zeros((aux_local, NT, tile_width, local_width), jnp.float32)
    virtual_sum = jnp.zeros((aux_local, local_width, NT, tile_width), jnp.float32)
    for slot in range(kcount):
        occupied_pick = occupied_all[source_rows[:, slot], slot]
        occupied_inputs = masked[:, source_rows[:, slot]]
        occupied_sum = occupied_sum + jnp.einsum(
            "tmn,ptml->ptnl", occupied_pick, occupied_inputs, preferred_element_type=jnp.float32
        )
        virtual_inputs = masked[:, partner_rows[:, slot]]
        virtual_sum = virtual_sum + jnp.einsum(
            "tnm,ptml->pltn",
            virtual_pick[:, slot],
            virtual_inputs,
            preferred_element_type=jnp.float32,
        )
    occupied_part = occupied_sum.astype(jnp.bfloat16)
    virtual_part = virtual_sum.astype(jnp.bfloat16).reshape(
        aux_local, local_tiles, tile_width, basis_size
    )
    occupied_moved = lax.all_to_all(occupied_part, "grp", split_axis=1, concat_axis=3, tiled=True)
    occupied_full, virtual_full = (
        lax.all_to_all(occupied_moved, "blk", split_axis=2, concat_axis=0, tiled=True),
        lax.all_to_all(virtual_part, "blk", split_axis=2, concat_axis=0, tiled=True),
    )
    left_side = occupied_full.reshape(occupied_full.shape[0], -1)
    right_side = virtual_full.reshape(virtual_full.shape[0], -1)
    partial_sum = jnp.einsum(
        "pe,qe->pq", left_side, right_side, preferred_element_type=jnp.float32
    ) * (1.0 / basis_size)
    total = lax.psum(partial_sum, ("grp", "blk"))
    return lax.dynamic_slice_in_dim(total, lax.axis_index("blk") * aux_local, aux_local, 0)


def solution(mesh):
    in_specs = (
        P("blk", None, "grp"),
        P(),
        P(),
        P(("grp", "blk"), None),
        P(),
        P(("grp", "blk"), None),
        P(),
    )
    out_specs = P("blk", None)
    return jax.shard_map(body, mesh=mesh, in_specs=in_specs, out_specs=out_specs, check_vma=False)
```

profile of v0, /device:TPU:1, one launch (start us, length us, event | category | flops | bytes accessed | tf_op | source)
XLA Modules:
  0.0 427.2 jit_solution(16286854891178512670)
XLA Ops:
  34.0 102.1 %all-gather.3.cloned.1.call-done = bf16[16384,128]{1,0:T(8,128)(2,1)} async-done(((bf16[32,128]{1,0:T(8,128)(2,1)}), bf16[16384,128]{1,0:T(8,128)(2,1)}) %all-gather.3.cloned.1.call-update) | async-done | bytes 4194320 | tf_op jit(solution)/shard_map/all_gather | solution.py:32
  136.1 3.6 gather_fusion.1
  139.7 3.6 gather_fusion.3
  143.3 3.6 gather_fusion.5
  146.9 3.6 gather_fusion.7
  150.5 2.9 gather_fusion.9
  153.4 2.8 gather_fusion.11
  156.2 2.8 gather_fusion.13
  159.1 2.8 gather_fusion.15
  162.0 1.7 fusion.25
  163.7 1.6 convolution_add_fusion.13
  168.3 6.0 %all-to-all-start = ((bf16[1,16,128,128]{2,3,0,1:T(8,128)(2,1)}), bf16[1,16,128,128]{2,3,0,1:T(8,128)(2,1)S(1)}, u32[]{:S(2)}, u32[]{:S(2)}) async-start(bf16[1,16,128,128]{2,3,0,1:T(8,128)(2,1)} %fusion.2), calls=%async_computation | async-start | bytes 1048576 | tf_op jit(solution)/shard_map/all_to_all | solution.py:59
  174.4 81.7 %all-gather.5.cloned.1.call-done = bf16[16384,128]{1,0:T(8,128)(2,1)} async-done(((bf16[32,128]{1,0:T(8,128)(2,1)}), bf16[16384,128]{1,0:T(8,128)(2,1)}) %all-gather.5.cloned.1.call-update) | async-done | bytes 4194320 | tf_op jit(solution)/shard_map/all_gather | solution.py:33
  256.1 5.4 %gather_fusion.17 = bf16[16,8,128,128]{3,2,1,0:T(8,128)(2,1)} fusion(bf16[16,8,128,128]{3,2,1,0:T(8,128)(2,1)} %bitcast.152, s32[1024]{0:T(1024)S(1)} %pad_clamp_fusion.8), kind=kCustom, calls=%fused_computation.17 | custom fusion | bytes 8388672 | tf_op jit(solution)/shard_map/gather | solution.py:39
  262.9 1.6 convolution_add_fusion.6
  268.0 3.7 reduce.6
  272.9 6.9 %all-to-all-start.2 = ((bf16[32,2,4096]{2,1,0:T(2,128)(2,1)}), bf16[32,2,4096]{2,1,0:T(2,128)(2,1)S(1)}, u32[]{:S(2)}, u32[]{:S(2)}) async-start(bf16[32,2,4096]{2,1,0:T(2,128)(2,1)} %reshape.405), calls=%async_computation.2 | async-start | bytes 1048576 | tf_op jit(solution)/shard_map/all_to_all | solution.py:62
  280.7 3.7 reduce.7
  285.6 10.8 %all-to-all-done.2 = bf16[32,2,4096]{2,1,0:T(2,128)(2,1)S(1)} async-done(((bf16[32,2,4096]{2,1,0:T(2,128)(2,1)}), bf16[32,2,4096]{2,1,0:T(2,128)(2,1)S(1)}, u32[]{:S(2)}, u32[]{:S(2)}) %all-to-all-start.2) | async-done | bytes 524320 | tf_op jit(solution)/shard_map/all_to_all | solution.py:62
  296.4 5.2 %all-to-all-start.1 = ((bf16[32,2,4096]{2,1,0:T(2,128)(2,1)}), bf16[32,2,4096]{2,1,0:T(2,128)(2,1)S(1)}, u32[]{:S(2)}, u32[]{:S(2)}) async-start(bf16[32,2,4096]{2,1,0:T(2,128)(2,1)} %reshape.407), calls=%async_computation.1 | async-start | bytes 1048576 | tf_op jit(solution)/shard_map/all_to_all | solution.py:61
  302.2 3.0 bitcast_reduce_fusion.1
  305.4 11.3 %all-to-all-done.1 = bf16[32,2,4096]{2,1,0:T(2,128)(2,1)S(1)} async-done(((bf16[32,2,4096]{2,1,0:T(2,128)(2,1)}), bf16[32,2,4096]{2,1,0:T(2,128)(2,1)S(1)}, u32[]{:S(2)}, u32[]{:S(2)}) %all-to-all-start.1) | async-done | bytes 524320 | tf_op jit(solution)/shard_map/all_to_all | solution.py:61
  317.2 3.0 bitcast_reduce_fusion
  321.6 98.2 %psum.7 = f32[32,32]{1,0:T(8,128)S(1)} all-reduce(f32[32,32]{1,0:T(8,128)S(1)} %fusion.3), channel_id=1, replica_groups=mesh['grp'=16,'blk'=32] {'grp','blk'}, use_global_device_ids=true, to_apply=%region_1.2 | all-reduce | flops 1024 | bytes 8192 | tf_op jit(solution)/shard_map/psum | solution.py:69
  (95 shorter events, 41.7 us)
Async XLA Ops:
  6.5 129.6 %all-gather.3.cloned.1.call-start = ((), (), s32[]{:S(2)}) async-start(), calls=%async_computation.3 | async-start | bytes 4202496 | tf_op jit(solution)/shard_map/all_gather | solution.py:32
  7.3 248.8 %all-gather.5.cloned.1.call-start = ((), (), s32[]{:S(2)}) async-start(), calls=%async_computation.4 | async-start | bytes 4202496 | tf_op jit(solution)/shard_map/all_gather | solution.py:33
  23.3 10.7 %copy-start.15 = (s32[16]{0:T(128)S(1)}, s32[16]{0:T(128)}, u32[]{:S(2)}) copy-start(s32[16]{0:T(128)} %param.9) | copy-start | bytes 196
  161.9 3.4 copy-start.2
  161.9 3.4 copy-start.11
  161.9 3.7 copy-start.1
  161.9 3.7 copy-start.10
  163.7 2.4 copy-start.13
  165.3 1.1 copy-start.12
  165.7 1.1 copy-start.14
  168.3 104.6 %all-to-all-start = ((bf16[1,16,128,128]{2,3,0,1:T(8,128)(2,1)}), bf16[1,16,128,128]{2,3,0,1:T(8,128)(2,1)S(1)}, u32[]{:S(2)}, u32[]{:S(2)}) async-start(bf16[1,16,128,128]{2,3,0,1:T(8,128)(2,1)} %fusion.2), calls=%async_computation | async-start | bytes 1048576 | tf_op jit(solution)/shard_map/all_to_all | solution.py:59
  256.1 5.4 %copy-start.3 = (bf16[16,128,128]{2,1,0:T(8,128)(2,1)S(1)}, bf16[16,128,128]{2,1,0:T(8,128)(2,1)}, u32[]{:S(2)}) copy-start(bf16[16,128,128]{2,1,0:T(8,128)(2,1)} %gather_fusion.16) | copy-start | bytes 1572868
  256.1 6.9 %copy-start.4 = (bf16[16,128,128]{2,1,0:T(8,128)(2,1)S(1)}, bf16[16,128,128]{2,1,0:T(8,128)(2,1)}, u32[]{:S(2)}) copy-start(bf16[16,128,128]{2,1,0:T(8,128)(2,1)} %gather_fusion.18) | copy-start | bytes 1572868
  261.4 3.1 copy-start
  261.4 3.1 copy-start.5
  261.4 3.4 copy-start.6
  262.9 2.2 copy-start.7
  264.5 1.1 copy-start.8
  264.8 1.1 copy-start.9
  272.9 23.5 %all-to-all-start.2 = ((bf16[32,2,4096]{2,1,0:T(2,128)(2,1)}), bf16[32,2,4096]{2,1,0:T(2,128)(2,1)S(1)}, u32[]{:S(2)}, u32[]{:S(2)}) async-start(bf16[32,2,4096]{2,1,0:T(2,128)(2,1)} %reshape.405), calls=%async_computation.2 | async-start | bytes 1048576 | tf_op jit(solution)/shard_map/all_to_all | solution.py:62
  296.4 20.3 %all-to-all-start.1 = ((bf16[32,2,4096]{2,1,0:T(2,128)(2,1)}), bf16[32,2,4096]{2,1,0:T(2,128)(2,1)S(1)}, u32[]{:S(2)}, u32[]{:S(2)}) async-start(bf16[32,2,4096]{2,1,0:T(2,128)(2,1)} %reshape.407), calls=%async_computation.1 | async-start | bytes 1048576 | tf_op jit(solution)/shard_map/all_to_all | solution.py:61
Sparse Core Ops, SparseCore 0:
  11.5 124.5 all-gather.2
  140.3 115.6 all-gather.4
where the time goes:
time: 428 us; the launch traced here: 427 us
  waiting for transfers between devices  207 us (48%)
  blocking collectives  98.2 us (23%)
  local copies, waits for them, and re-layouts  66.5 us (16%)
  starting transfers between devices  18.1 us (4%)
  between operations  13.9 us (3%)
  matrix products  12.2 us (3%)
  other arithmetic  10.9 us (3%)
    all_gather x1, waiting for transfers between devices, body(): lax.all_gather(occupied_tiles, ('grp', 'blk'), axis=0, tiled=True)  102 us
    psum x1, blocking collectives, body(): total = lax.psum(partial_sum, ('grp', 'blk'))  98.2 us
    all_gather x1, waiting for transfers between devices, body(): lax.all_gather(virtual_tiles, ('grp', 'blk'), axis=0, tiled=True)  81.7 us
    gather x8, local copies, waits for them, and re-layouts, body(): occupied_pick = occupied_all[source_rows[:, slot], slot]  25.8 us
    all_to_all x1, waiting for transfers between devices, body(): lax.all_to_all(occupied_moved, 'blk', split_axis=2, concat_axis=0, tiled=...  11.3 us
    all_to_all x1, waiting for transfers between devices, body(): lax.all_to_all(virtual_part, 'blk', split_axis=2, concat_axis=0, tiled=True)  10.8 us
    gather x8, local copies, waits for them, and re-layouts, body(): occupied_inputs = masked[:, source_rows[:, slot]]  10.6 us
    gather x8, local copies, waits for them, and re-layouts, body(): virtual_inputs = masked[:, partner_rows[:, slot]]  10.6 us
  transfers between devices with their start and end apart: 5, of which 4 were waited for; matrix products, arithmetic and copies ran while one was open for 20% of the time, Pallas kernels for 0%

commit v1 on v0

--- a/solution.py
+++ b/solution.py
@@ -66,7 +66,8 @@
     partial_sum = jnp.einsum(
         "pe,qe->pq", left_side, right_side, preferred_element_type=jnp.float32
     ) * (1.0 / basis_size)
-    total = lax.psum(partial_sum, ("grp", "blk"))
+    parts = lax.all_gather(partial_sum, ("grp", "blk"))
+    total = jnp.sum(parts, axis=0)
     return lax.dynamic_slice_in_dim(total, lax.axis_index("blk") * aux_local, aux_local, 0)
 
 

time: 428 us -> 459 us (1.072)
  waiting for transfers between devices: 207 us -> 332 us
  blocking collectives: 98.2 us -> 0 us
    all_gather x0 -> x1, waiting for transfers between devices: none -> 125 us  [body(): parts = lax.all_gather(partial_sum, ('grp', 'blk'))]
    psum x1 -> x0, blocking collectives: 98.2 us -> none  [body(): total = lax.psum(partial_sum, ('grp', 'blk'))]
  transfers between devices with their start and end apart: 5 -> 6, of which waited for: 4 -> 5; matrix products, arithmetic and copies ran while one was open for 20% -> 18% of each run, Pallas kernels for 0% -> 0%
where the time goes in v1:
time: 459 us; the launch traced here: 458 us
  waiting for transfers between devices  332 us (72%)
  local copies, waits for them, and re-layouts  66.6 us (15%)
  starting transfers between devices  18.2 us (4%)
  other arithmetic  14.9 us (3%)
  between operations  13.6 us (3%)
  matrix products  12.8 us (3%)
    all_gather x1, waiting for transfers between devices, body(): parts = lax.all_gather(partial_sum, ('grp', 'blk'))  125 us
    all_gather x1, waiting for transfers between devices, body(): lax.all_gather(occupied_tiles, ('grp', 'blk'), axis=0, tiled=True)  102 us
    all_gather x1, waiting for transfers between devices, body(): lax.all_gather(virtual_tiles, ('grp', 'blk'), axis=0, tiled=True)  81.7 us
    gather x8, local copies, waits for them, and re-layouts, body(): occupied_pick = occupied_all[source_rows[:, slot], slot]  25.8 us
    all_to_all x1, waiting for transfers between devices, body(): lax.all_to_all(occupied_moved, 'blk', split_axis=2, concat_axis=0, tiled=...  11.3 us
    all_to_all x1, waiting for transfers between devices, body(): lax.all_to_all(virtual_part, 'blk', split_axis=2, concat_axis=0, tiled=True)  10.8 us
    gather x8, local copies, waits for them, and re-layouts, body(): occupied_inputs = masked[:, source_rows[:, slot]]  10.6 us
    gather x8, local copies, waits for them, and re-layouts, body(): virtual_inputs = masked[:, partner_rows[:, slot]]  10.6 us
  transfers between devices with their start and end apart: 6, of which 5 were waited for; matrix products, arithmetic and copies ran while one was open for 18% of the time, Pallas kernels for 0%

profile of v1, /device:TPU:1, one launch (start us, length us, event | category | flops | bytes accessed | tf_op | source)
XLA Modules:
  0.0 458.1 jit_solution(11678950308730475279)
XLA Ops:
  34.0 102.1 %all-gather.5.cloned.1.call-done = bf16[16384,128]{1,0:T(8,128)(2,1)} async-done(((bf16[32,128]{1,0:T(8,128)(2,1)}), bf16[16384,128]{1,0:T(8,128)(2,1)}) %all-gather.5.cloned.1.call-update) | async-done | bytes 4194320 | tf_op jit(solution)/shard_map/all_gather | solution.py:32
  136.1 3.6 gather_fusion.1
  139.7 3.6 gather_fusion.3
  143.3 3.6 gather_fusion.5
  146.9 3.6 gather_fusion.7
  150.5 2.9 gather_fusion.9
  153.4 2.8 gather_fusion.11
  156.2 2.8 gather_fusion.13
  159.1 2.8 gather_fusion.15
  162.0 1.7 fusion.25
  168.3 6.0 %all-to-all-start = ((bf16[1,16,128,128]{2,3,0,1:T(8,128)(2,1)}), bf16[1,16,128,128]{2,3,0,1:T(8,128)(2,1)S(1)}, u32[]{:S(2)}, u32[]{:S(2)}) async-start(bf16[1,16,128,128]{2,3,0,1:T(8,128)(2,1)} %fusion.2), calls=%async_computation | async-start | bytes 1048576 | tf_op jit(solution)/shard_map/all_to_all | solution.py:59
  174.4 81.7 %all-gather.7.cloned.1.call-done = bf16[16384,128]{1,0:T(8,128)(2,1)} async-done(((bf16[32,128]{1,0:T(8,128)(2,1)}), bf16[16384,128]{1,0:T(8,128)(2,1)}) %all-gather.7.cloned.1.call-update) | async-done | bytes 4194320 | tf_op jit(solution)/shard_map/all_gather | solution.py:33
  256.1 5.4 %gather_fusion.17 = bf16[16,8,128,128]{3,2,1,0:T(8,128)(2,1)} fusion(bf16[16,8,128,128]{3,2,1,0:T(8,128)(2,1)} %bitcast.154, s32[1024]{0:T(1024)S(1)} %pad_clamp_fusion.8), kind=kCustom, calls=%fused_computation.17 | custom fusion | bytes 8388672 | tf_op jit(solution)/shard_map/gather | solution.py:39
  268.0 3.7 reduce.6
  272.9 6.9 %all-to-all-start.2 = ((bf16[32,2,4096]{2,1,0:T(2,128)(2,1)}), bf16[32,2,4096]{2,1,0:T(2,128)(2,1)S(1)}, u32[]{:S(2)}, u32[]{:S(2)}) async-start(bf16[32,2,4096]{2,1,0:T(2,128)(2,1)} %reshape.406), calls=%async_computation.2 | async-start | bytes 1048576 | tf_op jit(solution)/shard_map/all_to_all | solution.py:62
  280.7 3.7 reduce.7
  285.7 10.8 %all-to-all-done.2 = bf16[32,2,4096]{2,1,0:T(2,128)(2,1)S(1)} async-done(((bf16[32,2,4096]{2,1,0:T(2,128)(2,1)}), bf16[32,2,4096]{2,1,0:T(2,128)(2,1)S(1)}, u32[]{:S(2)}, u32[]{:S(2)}) %all-to-all-start.2) | async-done | bytes 524320 | tf_op jit(solution)/shard_map/all_to_all | solution.py:62
  296.4 5.0 %all-to-all-start.1 = ((bf16[32,2,4096]{2,1,0:T(2,128)(2,1)}), bf16[32,2,4096]{2,1,0:T(2,128)(2,1)S(1)}, u32[]{:S(2)}, u32[]{:S(2)}) async-start(bf16[32,2,4096]{2,1,0:T(2,128)(2,1)} %reshape.408), calls=%async_computation.1 | async-start | bytes 1048576 | tf_op jit(solution)/shard_map/all_to_all | solution.py:61
  302.2 3.0 bitcast_reduce_fusion.1
  305.4 11.3 %all-to-all-done.1 = bf16[32,2,4096]{2,1,0:T(2,128)(2,1)S(1)} async-done(((bf16[32,2,4096]{2,1,0:T(2,128)(2,1)}), bf16[32,2,4096]{2,1,0:T(2,128)(2,1)S(1)}, u32[]{:S(2)}, u32[]{:S(2)}) %all-to-all-start.1) | async-done | bytes 524320 | tf_op jit(solution)/shard_map/all_to_all | solution.py:61
  317.2 3.0 bitcast_reduce_fusion
  320.4 1.8 fusion.3
  322.3 124.8 %all-gather.9.cloned.1.call-done = f32[16384,32]{1,0:T(8,128)} async-done(((f32[32,32]{1,0:T(8,128)}), f32[16384,32]{1,0:T(8,128)}) %all-gather.9.cloned.1.call-update) | async-done | bytes 2097168 | tf_op jit(solution)/shard_map/all_gather | solution.py:69
  447.1 4.0 reduce_sum.19
  (98 shorter events, 44.0 us)
Async XLA Ops:
  6.5 129.6 %all-gather.5.cloned.1.call-start = ((), (), s32[]{:S(2)}) async-start(), calls=%async_computation.3 | async-start | bytes 4202496 | tf_op jit(solution)/shard_map/all_gather | solution.py:32
  7.3 248.8 %all-gather.7.cloned.1.call-start = ((), (), s32[]{:S(2)}) async-start(), calls=%async_computation.4 | async-start | bytes 4202496 | tf_op jit(solution)/shard_map/all_gather | solution.py:33
  23.3 10.6 %copy-start.15 = (s32[16]{0:T(128)S(1)}, s32[16]{0:T(128)}, u32[]{:S(2)}) copy-start(s32[16]{0:T(128)} %param.9) | copy-start | bytes 196
  161.9 3.4 copy-start.2
  161.9 3.4 copy-start.11
  161.9 3.7 copy-start.1
  162.0 3.7 copy-start.10
  163.7 2.4 copy-start.13
  165.3 1.1 copy-start.12
  165.7 1.1 copy-start.14
  168.3 104.6 %all-to-all-start = ((bf16[1,16,128,128]{2,3,0,1:T(8,128)(2,1)}), bf16[1,16,128,128]{2,3,0,1:T(8,128)(2,1)S(1)}, u32[]{:S(2)}, u32[]{:S(2)}) async-start(bf16[1,16,128,128]{2,3,0,1:T(8,128)(2,1)} %fusion.2), calls=%async_computation | async-start | bytes 1048576 | tf_op jit(solution)/shard_map/all_to_all | solution.py:59
  256.1 5.4 %copy-start.3 = (bf16[16,128,128]{2,1,0:T(8,128)(2,1)S(1)}, bf16[16,128,128]{2,1,0:T(8,128)(2,1)}, u32[]{:S(2)}) copy-start(bf16[16,128,128]{2,1,0:T(8,128)(2,1)} %gather_fusion.16) | copy-start | bytes 1572868
  256.1 6.9 %copy-start.4 = (bf16[16,128,128]{2,1,0:T(8,128)(2,1)S(1)}, bf16[16,128,128]{2,1,0:T(8,128)(2,1)}, u32[]{:S(2)}) copy-start(bf16[16,128,128]{2,1,0:T(8,128)(2,1)} %gather_fusion.18) | copy-start | bytes 1572868
  261.4 3.1 copy-start
  261.4 3.1 copy-start.5
  261.4 3.4 copy-start.6
  262.9 2.2 copy-start.7
  264.5 1.1 copy-start.8
  264.9 1.1 copy-start.9
  272.9 23.5 %all-to-all-start.2 = ((bf16[32,2,4096]{2,1,0:T(2,128)(2,1)}), bf16[32,2,4096]{2,1,0:T(2,128)(2,1)S(1)}, u32[]{:S(2)}, u32[]{:S(2)}) async-start(bf16[32,2,4096]{2,1,0:T(2,128)(2,1)} %reshape.406), calls=%async_computation.2 | async-start | bytes 1048576 | tf_op jit(solution)/shard_map/all_to_all | solution.py:62
  296.4 20.3 %all-to-all-start.1 = ((bf16[32,2,4096]{2,1,0:T(2,128)(2,1)}), bf16[32,2,4096]{2,1,0:T(2,128)(2,1)S(1)}, u32[]{:S(2)}, u32[]{:S(2)}) async-start(bf16[32,2,4096]{2,1,0:T(2,128)(2,1)} %reshape.408), calls=%async_computation.1 | async-start | bytes 1048576 | tf_op jit(solution)/shard_map/all_to_all | solution.py:61
  301.4 145.7 %all-gather.9.cloned.1.call-start = ((), (), s32[]{:S(2)}) async-start(), calls=%async_computation.5 | async-start | bytes 8404992 | tf_op jit(solution)/shard_map/all_gather | solution.py:69
Sparse Core Ops, SparseCore 0:
  11.5 124.5 all-gather.4
  140.3 115.7 all-gather.6
  322.4 124.6 all-gather.8
